TPU v7x, 128 devices: a whole 4x4x4 slice. The times are simulated.
128 devices in a mesh: gx: 8 (over z, core), gy: 16 (over x, y).
Axes of the slice: x: 4, y: 4, z: 4, core: 2. Of those that a mesh axis runs over, the one named last changes fastest.
Arguments:
- tokens: bfloat16 [4096, 4096], P(('gx', 'gy')), may hold values from -3 to 3
- attn_gain: bfloat16 [4096], replicated, may hold values from 0.099609375 to 1.8984375
- mlp_gain: bfloat16 [4096], replicated, may hold values from 0.099609375 to 1.8984375
- w_query: bfloat16 [4096, 4096], P('gx', 'gy'), may hold values from -1 to 1
- w_key: bfloat16 [4096, 1024], P('gx', 'gy'), may hold values from -1 to 1
- value_projection: bfloat16 [4096, 1024], P('gx', 'gy'), may hold values from -0.09375 to 0.09375
- w_out: bfloat16 [4096, 4096], P('gy', 'gx'), may hold values from -0.09375 to 0.09375
- w_gate: bfloat16 [4096, 14336], P('gx', 'gy'), may hold values from -0.09375 to 0.09375
- w_up: bfloat16 [4096, 14336], P('gx', 'gy'), may hold values from -0.09375 to 0.09375
- w_down: bfloat16 [14336, 4096], P('gy', 'gx'), may hold values from -0.046875 to 0.046875
- lengths: int32 [6], replicated, may hold values from 1 to 3072, 4096 in all
- page_table: int32 [128, 2], replicated, may hold values from 0 to 15, as said below
Outputs:
- layer_out: bfloat16 [4096, 4096], P(('gx', 'gy'))
- paged_key_value_cache: bfloat16 [128, 2, 32, 1024], P('gx', None, None, 'gy')
Inputs may be any that keep to these rules, and one draw needn't show every extreme that they name: `page_table`: page p belongs to token group p // 16, the tokens of one index of gx. Its owner is an index of gx and its slot is below 16; every pair of owner and slot is taken by exactly one page. Of one token group's pages, 8 owners receive exactly 2 each and the other owners none.
All inputs are finite; a program needn't handle non-finite values.
Results may differ from a plain program's by a relative error of at most 0.025.
The roundings to bfloat16 on the way count: a program that leaves them out, or rounds other values in their place, can miss the bound.
Values may be sent and summed in bfloat16 or wider, within the bound.
A program may use at most 128 MiB of HBM per device.

v0:
```python
import jax
import jax.numpy as jnp
from jax import lax
from jax.sharding import PartitionSpec as P

HEAD_WIDTH = 128
WIN = 4096
PAGE_TOKENS = 32
rope_base = 10000.0
norm_eps = 1e-05
masked_score = -1e30


def partner(value, axis, distance):
    mask = 2**distance
    pairs = [(source, source ^ mask) for source in range(lax.axis_size(axis))]
    return lax.ppermute(value, axis, pairs)


def rms_scale(values, gain):
    floats = values.astype(jnp.float32)
    mean_square = jnp.mean(floats * floats, axis=-1, keepdims=True)
    return floats * lax.rsqrt(mean_square + norm_eps) * gain.astype(jnp.float32)


def segment_info(lengths, token_index):
    ends = jnp.cumsum(lengths, dtype=jnp.int32)
    starts = ends - lengths
    inside = (token_index[:, None] >= starts[None, :]).astype(jnp.int32)
    segment = jnp.sum(inside, axis=1, dtype=jnp.int32) - 1
    chosen = (segment[:, None] == jnp.arange(lengths.shape[0], dtype=jnp.int32)[None, :]).astype(
        jnp.int32
    )
    token_positions = token_index - jnp.sum(chosen * starts[None, :], axis=1, dtype=jnp.int32)
    return (segment, token_positions)


def apply_rotary(values, token_positions):
    half = values.shape[-1] // 2
    freq = rope_base ** (-jnp.arange(half, dtype=jnp.float32) * 2.0 / values.shape[-1])
    angle = token_positions.astype(jnp.float32)[:, None] * freq[None, :]
    cosine = jnp.cos(angle)[:, None, :]
    sine = jnp.sin(angle)[:, None, :]
    first = values[..., :half]
    second = values[..., half:]
    return jnp.concatenate(
        [first * cosine - second * sine, second * cosine + first * sine], axis=-1
    )


def join_halves(mine, other, lower):
    return jnp.where(
        lower, jnp.concatenate([mine, other], axis=1), jnp.concatenate([other, mine], axis=1)
    )


def row_products(source, pieces):
    return tuple((jnp.dot(source, piece, preferred_element_type=jnp.float32) for piece in pieces))


def per_device(
    tokens,
    attn_gain,
    mlp_gain,
    w_query,
    w_key,
    value_projection,
    w_out,
    w_gate,
    w_up,
    w_down,
    lengths,
    page_table,
):
    group_count = lax.axis_size("gx")
    local_rows = tokens.shape[0]
    group = local_rows * lax.axis_size("gy")
    group_index = lax.axis_index("gx")
    head_index = lax.axis_index("gy")
    group_start = group_index * group
    lower = head_index % 2 == 0
    query_cols = w_query.shape[1]
    query_heads = query_cols // HEAD_WIDTH
    key_cols = w_key.shape[1]
    key_heads = max(1, key_cols // HEAD_WIDTH)
    per_key = query_heads // key_heads
    normed = lax.all_gather(
        rms_scale(tokens, attn_gain).astype(jnp.bfloat16), "gy", axis=0, tiled=True
    )
    query = row_products(normed, (lax.all_gather(w_query, "gx", axis=0, tiled=True),))[0]
    key_weight, value_weight = (w_key, value_projection)
    unrotated_key, value_raw = row_products(
        normed,
        (
            lax.all_gather(key_weight, "gx", axis=0, tiled=True),
            lax.all_gather(value_weight, "gx", axis=0, tiled=True),
        ),
    )
    other_key, other_value = (
        partner(unrotated_key.astype(jnp.bfloat16), "gy", 0).astype(unrotated_key.dtype),
        partner(value_raw.astype(jnp.bfloat16), "gy", 0).astype(value_raw.dtype),
    )
    unrotated_key = join_halves(unrotated_key, other_key, lower)
    value_raw = join_halves(value_raw, other_value, lower)
    token_index = group_start + jnp.arange(group, dtype=jnp.int32)
    segment, token_positions = segment_info(lengths, token_index)
    query_rot = (
        apply_rotary(query.reshape(group, query_heads, HEAD_WIDTH), token_positions)
        .astype(jnp.bfloat16)
        .reshape(group, key_heads, per_key, HEAD_WIDTH)
    )
    rotated_key = (
        apply_rotary(unrotated_key.reshape(group, key_heads, HEAD_WIDTH), token_positions)
        .astype(jnp.bfloat16)
        .reshape(group, key_heads * HEAD_WIDTH)
    )
    value_vectors = value_raw.astype(jnp.bfloat16)
    scale = HEAD_WIDTH ** (-0.5)
    start_state = (
        jnp.full((key_heads, per_key, group), masked_score, jnp.float32),
        jnp.zeros((key_heads, per_key, group), jnp.float32),
        jnp.zeros((key_heads, per_key, group, HEAD_WIDTH), jnp.float32),
    )
    keys = lax.all_gather(rotated_key, "gx", axis=0, tiled=True)
    values = lax.all_gather(value_vectors, "gx", axis=0, tiled=True)
    count = keys.shape[0]
    key_index = jnp.arange(count, dtype=jnp.int32)
    key_segment, unused = segment_info(lengths, key_index)
    distance = token_index[:, None] - key_index[None, :]
    allowed = (segment[:, None] == key_segment[None, :]) & (distance >= 0) & (distance < WIN)

    def update(state):
        running, total, weighted = state
        scores = (
            jnp.einsum(
                "qhgd,khd->hgqk",
                query_rot,
                keys.reshape(count, key_heads, HEAD_WIDTH),
                preferred_element_type=jnp.float32,
            )
            * scale
        )
        masked = jnp.where(allowed[None, None], scores, masked_score)
        newest = jnp.maximum(running, jnp.max(masked, axis=-1))
        weights = jnp.where(allowed[None, None], jnp.exp(masked - newest[..., None]), 0.0)
        mixed = jnp.einsum(
            "hgqk,khd->hgqd",
            weights.astype(jnp.bfloat16),
            values.reshape(count, key_heads, HEAD_WIDTH),
            preferred_element_type=jnp.float32,
        )
        return (newest, jnp.sum(weights, axis=-1), mixed)

    state = lax.cond(jnp.any(allowed), update, lambda state: state, start_state)
    attended = (state[2] / state[1][..., None]).astype(jnp.bfloat16)
    attended = attended.transpose(2, 0, 1, 3).reshape(group, query_cols)
    partial_value = jnp.dot(
        attended,
        lax.all_gather(w_out, "gx", axis=1, tiled=True),
        preferred_element_type=jnp.float32,
    )
    share = lax.psum_scatter(
        partial_value.astype(jnp.bfloat16), "gy", scatter_dimension=0, tiled=True
    ).astype(jnp.float32)
    residual = (tokens.astype(jnp.float32) + share).astype(jnp.bfloat16)
    mlp_input = lax.all_gather(
        rms_scale(residual, mlp_gain).astype(jnp.bfloat16), "gy", axis=0, tiled=True
    )
    gate, up_values = row_products(
        mlp_input,
        (
            lax.all_gather(w_gate, "gx", axis=0, tiled=True),
            lax.all_gather(w_up, "gx", axis=0, tiled=True),
        ),
    )
    hidden = (jax.nn.silu(gate) * up_values).astype(jnp.bfloat16)
    down_full = lax.all_gather(w_down, "gx", axis=1, tiled=True)
    mlp_share = lax.psum_scatter(
        jnp.dot(hidden, down_full, preferred_element_type=jnp.float32).astype(jnp.bfloat16),
        "gy",
        scatter_dimension=0,
        tiled=True,
    ).astype(jnp.float32)
    layer_out = (residual.astype(jnp.float32) + mlp_share).astype(jnp.bfloat16)
    own_start = jnp.where(lower, 0, key_cols).astype(jnp.int32)
    local_key = lax.dynamic_slice_in_dim(rotated_key, own_start, key_cols, 1)
    own_value = lax.dynamic_slice_in_dim(value_vectors, own_start, key_cols, 1)
    slots_group = group // PAGE_TOKENS
    capacity = max(2, slots_group // group_count)
    pages_local = (
        jnp.stack([local_key, own_value], axis=0)
        .reshape(2, slots_group, PAGE_TOKENS, key_cols)
        .transpose(1, 0, 2, 3)
        .reshape(slots_group, 2 * PAGE_TOKENS * key_cols)
    )
    owner = page_table[:, 0]
    slot = page_table[:, 1]
    page_index = jnp.arange(owner.shape[0], dtype=jnp.int32)
    page_group = page_index // slots_group
    before = (
        (page_group[:, None] == page_group[None, :])
        & (owner[:, None] == owner[None, :])
        & (page_index[None, :] < page_index[:, None])
    )
    rank = jnp.sum(before.astype(jnp.int32), axis=1, dtype=jnp.int32)
    my_owner = lax.dynamic_slice_in_dim(owner, group_index * slots_group, slots_group, 0)
    my_rank = lax.dynamic_slice_in_dim(rank, group_index * slots_group, slots_group, 0)
    target = jnp.arange(group_count * capacity, dtype=jnp.int32)
    select = (
        (my_owner[None, :] == target[:, None] // capacity)
        & (my_rank[None, :] == target[:, None] % capacity)
    ).astype(jnp.bfloat16)
    outgoing = (
        jnp.dot(select, pages_local, preferred_element_type=jnp.float32)
        .astype(jnp.bfloat16)
        .reshape(group_count, capacity, 2, PAGE_TOKENS, key_cols)
    )
    incoming = lax.all_to_all(outgoing, "gx", split_axis=0, concat_axis=0, tiled=True)
    column = page_group * capacity + rank
    pick = (
        (owner[None, :] == group_index)
        & (slot[None, :] == jnp.arange(slots_group, dtype=jnp.int32)[:, None])
    ).astype(jnp.float32)
    place = (column[:, None] == target[None, :]).astype(jnp.float32)
    routing = jnp.dot(pick, place, preferred_element_type=jnp.float32).astype(jnp.bfloat16)
    paged_key_value_cache = (
        jnp.dot(
            routing,
            incoming.reshape(group_count * capacity, 2 * PAGE_TOKENS * key_cols),
            preferred_element_type=jnp.float32,
        )
        .astype(jnp.bfloat16)
        .reshape(slots_group, 2, PAGE_TOKENS, key_cols)
    )
    return (layer_out, paged_key_value_cache)


def solution(mesh):
    placed = (
        P(("gx", "gy"), None),
        P(),
        P(),
        P("gx", "gy"),
        P("gx", "gy"),
        P("gx", "gy"),
        P("gy", "gx"),
        P("gx", "gy"),
        P("gx", "gy"),
        P("gy", "gx"),
        P(),
        P(),
    )
    return jax.shard_map(
        per_device,
        mesh=mesh,
        in_specs=placed,
        out_specs=(P(("gx", "gy"), None), P("gx", None, None, "gy")),
        check_vma=False,
    )
```

profile of v0, /device:TPU:0, one launch (start us, length us, event | category | flops | bytes accessed | tf_op | source)
XLA Modules:
  0.0 550.2 jit_solution(15981981439846609788)
XLA Ops:
  7.2 0.7 convert_element_type.115
  7.9 1.1 fusion.21
  9.1 1.8 fusion.23
  10.9 0.7 all-gather.12.cloned.1.call-update
  11.7 0.8 reduce-window.9
  12.5 0.7 bitcast_subtract_fusion
  13.4 14.6 %all_gather.35 = bf16[4096,64]{0,1:T(8,128)(2,1)S(1)} all-gather(bf16[512,64]{0,1:T(8,128)(2,1)} %param.18), channel_id=1, replica_groups=mesh['gx'=8,'gy'=16] {'gx'}, dimensions={0}, use_global_device_ids=true | all-gather | bytes 589824 | tf_op jit(solution)/shard_map/all_gather | solution.py:95
  28.0 36.9 %all-gather.10.cloned.1.call-done = bf16[512,4096]{1,0:T(8,128)(2,1)} async-done(((bf16[32,4096]{1,0:T(8,128)(2,1)}), bf16[512,4096]{1,0:T(8,128)(2,1)}) %all-gather.10.cloned.1.call-update) | async-done | bytes 4194320 | tf_op jit(solution)/shard_map/all_gather | solution.py:87
  64.9 3.6 fusion.62
  68.5 1.5 collective-permute-start
  70.0 2.8 collective-permute-done
  72.9 0.6 fusion.37
  73.4 0.7 pad_maximum_fusion.1
  74.2 14.2 %all_gather.37 = bf16[4096,64]{0,1:T(8,128)(2,1)S(1)} all-gather(bf16[512,64]{0,1:T(8,128)(2,1)S(1)} %copy-done.3), channel_id=1, replica_groups=mesh['gx'=8,'gy'=16] {'gx'}, dimensions={0}, use_global_device_ids=true | all-gather | bytes 589824 | tf_op jit(solution)/shard_map/all_gather | solution.py:96
  88.3 3.7 fusion.64
  92.0 1.8 collective-permute-start.1
  93.8 2.6 collective-permute-done.1
  96.4 0.7 fusion.31
  97.9 3.6 fusion.20
  102.1 1.8 multiply_cosine_fusion
  103.9 4.2 fusion.63
  108.5 1.2 fusion.29
  109.9 7.8 %all-gather.14.cloned.1.call-done = bf16[4096,128]{0,1:T(8,128)(2,1)} async-done(((bf16[512,128]{0,1:T(8,128)(2,1)}), bf16[4096,128]{0,1:T(8,128)(2,1)}) %all-gather.14.cloned.1.call-update) | async-done | bytes 1048592 | tf_op jit(solution)/shard_map/all_gather | solution.py:124
  117.7 25.0 %all-gather.16.cloned.1.call-done = bf16[4096,128]{0,1:T(8,128)(2,1)} async-done(((bf16[512,128]{0,1:T(8,128)(2,1)}), bf16[4096,128]{0,1:T(8,128)(2,1)}) %all-gather.16.cloned.1.call-update) | async-done | bytes 1048592 | tf_op jit(solution)/shard_map/all_gather | solution.py:125
  142.8 14.2 %conditional.1 = (f32[1,2,512]{2,1,0:T(2,128)S(1)}, f32[1,2,512,128]{2,3,1,0:T(8,128)S(1)}) conditional(s32[]{:T(128)} %convert_element_type.114, () %tuple.16, (pred[512,4096]{0,1:T(8,128)(4,1)S(1)}, bf16[512,1,2,128]{3,0,2,1:T(8,128)(2,1)S(1)}, bf16[4096,128]{0,1:T(8,128)(2,1)}, bf16[4096,128]{0,1:T(8,128)(2,1)}) %tuple.17), branch_computations={%region_6.7_spmd, %region_7.10_spmd} | conditional | flops 2202008576 | bytes 63725612 | solution.py:154
  142.8 5.1 fusion
  147.9 4.6 fusion.7
  152.5 4.4 fusion.2
  157.0 12.6 %all-gather.18.cloned.1.call-done = bf16[256,4096]{1,0:T(8,128)(2,1)} async-done(((bf16[256,512]{1,0:T(8,128)(2,1)}), bf16[256,4096]{1,0:T(8,128)(2,1)}) %all-gather.18.cloned.1.call-update) | async-done | bytes 2097168 | tf_op jit(solution)/shard_map/all_gather | solution.py:159
  169.6 4.9 convolution_convert_fusion.1
  174.6 0.7 all-gather.22.cloned.1.call-update
  175.4 77.2 %reduce-scatter.3.cloned.1.call-done = bf16[32,4096]{1,0:T(8,128)(2,1)} async-done(((bf16[512,4096]{1,0:T(8,128)(2,1)}), bf16[32,4096]{1,0:T(8,128)(2,1)}) %reduce-scatter.3.cloned.1.call-update) | async-done | bytes 262160 | tf_op jit(solution)/shard_map/reduce_scatter | solution.py:162
  252.6 1.1 fusion.25
  253.7 1.8 fusion.27
  255.6 0.7 all-gather.24.cloned.1.call-update
  257.1 42.2 %all-gather.22.cloned.1.call-done = bf16[4096,896]{1,0:T(8,128)(2,1)} async-done(((bf16[512,896]{1,0:T(8,128)(2,1)}), bf16[4096,896]{1,0:T(8,128)(2,1)}) %all-gather.22.cloned.1.call-update) | async-done | bytes 7340048 | tf_op jit(solution)/shard_map/all_gather | solution.py:172
  299.4 54.3 %all-gather.20.cloned.1.call-done = bf16[512,4096]{1,0:T(8,128)(2,1)} async-done(((bf16[32,4096]{1,0:T(8,128)(2,1)}), bf16[512,4096]{1,0:T(8,128)(2,1)}) %all-gather.20.cloned.1.call-update) | async-done | bytes 4194320 | tf_op jit(solution)/shard_map/all_gather | solution.py:166
  353.7 9.8 %fusion.65 = f32[512,896]{1,0:T(8,128)S(1)} fusion(bf16[512,4096]{1,0:T(8,128)(2,1)} %all-gather.20.cloned.1.call-done, bf16[4096,896]{1,0:T(8,128)(2,1)} %all-gather.22.cloned.1.call-done), kind=kOutput, calls=%fused_computation.120 | convolution fusion | flops 3758096384 | bytes 13369344 | tf_op jit(solution)/shard_map/dot_general | solution.py:58
  363.5 37.2 %all-gather.24.cloned.1.call-done = bf16[4096,896]{1,0:T(8,128)(2,1)} async-done(((bf16[512,896]{1,0:T(8,128)(2,1)}), bf16[4096,896]{1,0:T(8,128)(2,1)}) %all-gather.24.cloned.1.call-update) | async-done | bytes 7340048 | tf_op jit(solution)/shard_map/all_gather | solution.py:173
  400.8 47.2 %all-gather.26.cloned.1.call-done = bf16[896,4096]{1,0:T(8,128)(2,1)} async-done(((bf16[896,512]{1,0:T(8,128)(2,1)}), bf16[896,4096]{1,0:T(8,128)(2,1)}) %all-gather.26.cloned.1.call-update) | async-done | bytes 7340048 | tf_op jit(solution)/shard_map/all_gather | solution.py:177
  448.0 16.3 %convolution_convert_fusion = bf16[512,4096]{1,0:T(8,128)(2,1)} fusion(bf16[896,4096]{1,0:T(8,128)(2,1)} %all-gather.26.cloned.1.call-done, f32[512,896]{1,0:T(8,128)S(1)} %fusion.65, bf16[512,4096]{1,0:T(8,128)(2,1)} %all-gather.20.cloned.1.call-done, bf16[4096,896]{1,0:T(8,128)(2,1)} %all-gather.24.cloned.1.call-done), kind=kOutput, calls=%fused_computation.22 | convolution fusion | flops 7521042432 | bytes 24903680 | tf_op jit(solution)/shard_map/dot_general | solution.py:179
  464.3 0.6 copy-done.5
  466.5 0.9 reshape.453
  467.4 3.4 all-to-all-start
  470.7 6.0 %all-to-all-done = bf16[8,2,4096]{2,1,0:T(2,128)(2,1)S(1)} async-done(((bf16[8,2,4096]{2,1,0:T(2,128)(2,1)}), bf16[8,2,4096]{2,1,0:T(2,128)(2,1)S(1)}, u32[]{:S(2)}, u32[]{:S(2)}) %all-to-all-start) | async-done | bytes 131104 | tf_op jit(solution)/shard_map/all_to_all | solution.py:218
  477.7 1.0 reshape.449
  478.6 63.3 %reduce-scatter.5.cloned.1.call-done = bf16[32,4096]{1,0:T(8,128)(2,1)} async-done(((bf16[512,4096]{1,0:T(8,128)(2,1)}), bf16[32,4096]{1,0:T(8,128)(2,1)}) %reduce-scatter.5.cloned.1.call-update) | async-done | bytes 262160 | tf_op jit(solution)/shard_map/reduce_scatter | solution.py:178
  541.9 1.7 fusion.28
  (72 shorter events, 5.2 us)
Async XLA Ops:
  7.2 57.7 %all-gather.10.cloned.1.call-start = ((), (), s32[]{:S(2)}) async-start(), calls=%async_computation.3 | async-start | bytes 4456448 | tf_op jit(solution)/shard_map/all_gather | solution.py:87
  7.9 66.3 %copy-start.3 = (bf16[512,64]{0,1:T(8,128)(2,1)S(1)}, bf16[512,64]{0,1:T(8,128)(2,1)}, u32[]{:S(2)}) copy-start(bf16[512,64]{0,1:T(8,128)(2,1)} %param.19) | copy-start | bytes 196612
  10.9 93.0 %all-gather.12.cloned.1.call-start = ((), (), s32[]{:S(2)}) async-start(), calls=%async_computation.4 | async-start | bytes 2359296 | tf_op jit(solution)/shard_map/all_gather | solution.py:90
  11.6 106.1 %all-gather.14.cloned.1.call-start = ((), (), s32[]{:S(2)}) async-start(), calls=%async_computation.5 | async-start | bytes 1179648 | tf_op jit(solution)/shard_map/all_gather | solution.py:124
  68.5 4.3 collective-permute-start
  74.1 68.7 %all-gather.16.cloned.1.call-start = ((), (), s32[]{:S(2)}) async-start(), calls=%async_computation.6 | async-start | bytes 1179648 | tf_op jit(solution)/shard_map/all_gather | solution.py:125
  92.0 4.4 collective-permute-start.1
  97.1 72.5 %all-gather.18.cloned.1.call-start = ((), (), s32[]{:S(2)}) async-start(), calls=%async_computation.7 | async-start | bytes 2359296 | tf_op jit(solution)/shard_map/all_gather | solution.py:159
  97.7 154.9 %reduce-scatter.3.cloned.1.call-start = ((), (), s32[]{:S(2)}) async-start(), calls=%async_computation.8 | async-start | bytes 4456448 | tf_op jit(solution)/shard_map/reduce_scatter | solution.py:162
  142.8 5.2 copy-start.6
  174.6 0.8 copy-start.4
  174.6 78.0 %copy-start = (bf16[32,4096]{1,0:T(8,128)(2,1)S(1)}, bf16[32,4096]{1,0:T(8,128)(2,1)}, u32[]{:S(2)}) copy-start(bf16[32,4096]{1,0:T(8,128)(2,1)} %param.14) | copy-start | bytes 786436
  174.6 124.8 %all-gather.22.cloned.1.call-start = ((), (), s32[]{:S(2)}) async-start(), calls=%async_computation.10 | async-start | bytes 8257536 | tf_op jit(solution)/shard_map/all_gather | solution.py:172
  175.3 178.4 %all-gather.20.cloned.1.call-start = ((), (), s32[]{:S(2)}) async-start(), calls=%async_computation.9 | async-start | bytes 4456448 | tf_op jit(solution)/shard_map/all_gather | solution.py:166
  255.5 145.2 %all-gather.24.cloned.1.call-start = ((), (), s32[]{:S(2)}) async-start(), calls=%async_computation.11 | async-start | bytes 8257536 | tf_op jit(solution)/shard_map/all_gather | solution.py:173
  256.3 191.7 %all-gather.26.cloned.1.call-start = ((), (), s32[]{:S(2)}) async-start(), calls=%async_computation.12 | async-start | bytes 8257536 | tf_op jit(solution)/shard_map/all_gather | solution.py:177
  256.9 285.0 %reduce-scatter.5.cloned.1.call-start = ((), (), s32[]{:S(2)}) async-start(), calls=%async_computation.13 | async-start | bytes 4456448 | tf_op jit(solution)/shard_map/reduce_scatter | solution.py:178
  464.2 0.7 copy-start.5
  464.2 1.2 copy-start.2
  464.2 77.7 %copy-start.1 = (bf16[32,4096]{1,0:T(8,128)(2,1)S(1)}, bf16[32,4096]{1,0:T(8,128)(2,1)}, u32[]{:S(2)}) copy-start(bf16[32,4096]{1,0:T(8,128)(2,1)} %reduce-scatter.3.cloned.1.call-done) | copy-start | bytes 786436
  467.4 9.4 %all-to-all-start = ((bf16[8,2,4096]{2,1,0:T(2,128)(2,1)}), bf16[8,2,4096]{2,1,0:T(2,128)(2,1)S(1)}, u32[]{:S(2)}, u32[]{:S(2)}) async-start(bf16[8,2,4096]{2,1,0:T(2,128)(2,1)} %reshape.453), calls=%async_computation.2 | async-start | bytes 262144 | tf_op jit(solution)/shard_map/all_to_all | solution.py:218
Sparse Core Ops, SparseCore 0:
  11.0 53.8 all-gather.9
  66.6 25.7 all-gather.11
  94.1 23.5 all-gather.13
  119.3 23.4 all-gather.15
  144.3 25.2 all-gather.17
  174.7 77.8 reduce-scatter.2
  254.4 44.9 all-gather.21
  302.3 51.3 all-gather.19
  355.5 45.2 all-gather.23
  402.4 45.4 all-gather.25
  464.4 77.4 reduce-scatter.4
where the time goes:
time: 551 us; the launch traced here: 550 us
  waiting for transfers between devices  419 us (76%)
  matrix products  52.7 us (10%)
  blocking collectives  28.8 us (5%)
  other arithmetic  23.6 us (4%)
  between operations  14.8 us (3%)
  starting transfers between devices  7.29 us (1%)
    reduce_scatter x1, waiting for transfers between devices, per_device(): lax.psum_scatter(partial_value.astype(jnp.bfloat16), 'gy', scatter_dimens...  77.2 us
    reduce_scatter x1, waiting for transfers between devices, per_device(): lax.psum_scatter(jnp.dot(hidden, down_full, preferred_element_type=jnp.fl...  63.3 us
    all_gather x1, waiting for transfers between devices, per_device(): lax.all_gather(rms_scale(residual, mlp_gain).astype(jnp.bfloat16), 'gy',...  54.3 us
    all_gather x1, waiting for transfers between devices, per_device(): down_full = lax.all_gather(w_down, 'gx', axis=1, tiled=True)  47.2 us
    all_gather x1, waiting for transfers between devices, per_device(): lax.all_gather(w_gate, 'gx', axis=0, tiled=True)  42.2 us
    all_gather x1, waiting for transfers between devices, per_device(): lax.all_gather(w_up, 'gx', axis=0, tiled=True)  37.2 us
    all_gather x1, waiting for transfers between devices, per_device(): lax.all_gather(rms_scale(tokens, attn_gain).astype(jnp.bfloat16), 'gy', a...  36.9 us
    all_gather x1, waiting for transfers between devices, per_device(): values = lax.all_gather(value_vectors, 'gx', axis=0, tiled=True)  25 us
  transfers between devices with their start and end apart: 14, of which 13 were waited for; matrix products, arithmetic and copies ran while one was open for 10% of the time, Pallas kernels for 0%

commit v1 on v0

--- a/solution.py
+++ b/solution.py
@@ -122,7 +122,12 @@
         jnp.zeros((key_heads, per_key, group, HEAD_WIDTH), jnp.float32),
     )
     keys = lax.all_gather(rotated_key, "gx", axis=0, tiled=True)
-    values = lax.all_gather(value_vectors, "gx", axis=0, tiled=True)
+    ring = [value_vectors]
+    for hop in range(7):
+        ring.append(lax.ppermute(ring[-1], "gx", [(dev, (dev + 1) % 8) for dev in range(8)]))
+    values = jnp.roll(
+        jnp.concatenate(ring[::-1], axis=0), (lax.axis_index("gx") + 1) * ring[0].shape[0], axis=0
+    )
     count = keys.shape[0]
     key_index = jnp.arange(count, dtype=jnp.int32)
     key_segment, unused = segment_info(lengths, key_index)

time: 551 us -> 562 us (1.020)
  local copies, waits for them, and re-layouts: 4.37 us -> 25.9 us
  waiting for transfers between devices: 419 us -> 401 us
  matrix products: 52.7 us -> 59.9 us
    ppermute x0 -> x7, waiting for transfers between devices: none -> 31.8 us  [per_device(): lax.ppermute(ring[-1], 'gx', [(dev, (dev + 1) % 8) for dev in range(8)])]
    all_gather x1 -> x0, waiting for transfers between devices: 25 us -> none  [per_device(): values = lax.all_gather(value_vectors, 'gx', axis=0, tiled=True)]
    unnamed x16 -> x53, local copies, waits for them, and re-layouts: 2.16 us -> 16.6 us
    all_gather x1, waiting for transfers between devices: 12.6 us -> 0.02 us  [per_device(): lax.all_gather(w_out, 'gx', axis=1, tiled=True)]
    all_gather x1, waiting for transfers between devices: 7.85 us -> 0.01 us  [per_device(): keys = lax.all_gather(rotated_key, 'gx', axis=0, tiled=True)]
  transfers between devices with their start and end apart: 14 -> 20, of which waited for: 13 -> 17; matrix products, arithmetic and copies ran while one was open for 10% -> 14% of each run, Pallas kernels for 0% -> 0%
where the time goes in v1:
time: 562 us; the launch traced here: 561 us
  waiting for transfers between devices  401 us (71%)
  matrix products  59.9 us (11%)
  blocking collectives  28.9 us (5%)
  local copies, waits for them, and re-layouts  25.9 us (5%)
  other arithmetic  22.9 us (4%)
  between operations  15.2 us (3%)
  starting transfers between devices  7.02 us (1%)
    reduce_scatter x1, waiting for transfers between devices, per_device(): lax.psum_scatter(partial_value.astype(jnp.bfloat16), 'gy', scatter_dimens...  73.6 us
    reduce_scatter x1, waiting for transfers between devices, per_device(): lax.psum_scatter(jnp.dot(hidden, down_full, preferred_element_type=jnp.fl...  63.3 us
    all_gather x1, waiting for transfers between devices, per_device(): lax.all_gather(rms_scale(residual, mlp_gain).astype(jnp.bfloat16), 'gy',...  54.3 us
    all_gather x1, waiting for transfers between devices, per_device(): down_full = lax.all_gather(w_down, 'gx', axis=1, tiled=True)  47.3 us
    all_gather x1, waiting for transfers between devices, per_device(): lax.all_gather(w_gate, 'gx', axis=0, tiled=True)  41.9 us
    all_gather x1, waiting for transfers between devices, per_device(): lax.all_gather(w_up, 'gx', axis=0, tiled=True)  37.3 us
    all_gather x1, waiting for transfers between devices, per_device(): lax.all_gather(rms_scale(tokens, attn_gain).astype(jnp.bfloat16), 'gy', a...  36.9 us
    ppermute x7, waiting for transfers between devices, per_device(): lax.ppermute(ring[-1], 'gx', [(dev, (dev + 1) % 8) for dev in range(8)])  31.8 us
  transfers between devices with their start and end apart: 20, of which 17 were waited for; matrix products, arithmetic and copies ran while one was open for 14% of the time, Pallas kernels for 0%

profile of v1, /device:TPU:0, one launch (start us, length us, event | category | flops | bytes accessed | tf_op | source)
XLA Modules:
  0.0 560.9 jit_solution(11295659468666818398)
XLA Ops:
  7.9 1.1 fusion.23
  9.0 1.8 fusion.25
  13.3 14.6 %all_gather.32 = bf16[4096,64]{0,1:T(8,128)(2,1)S(1)} all-gather(bf16[512,64]{0,1:T(8,128)(2,1)} %param.18), channel_id=1, replica_groups=mesh['gx'=8,'gy'=16] {'gx'}, dimensions={0}, use_global_device_ids=true | all-gather | bytes 589824 | tf_op jit(solution)/shard_map/all_gather | solution.py:95
  27.9 36.9 %all-gather.9.cloned.1.call-done = bf16[512,4096]{1,0:T(8,128)(2,1)} async-done(((bf16[32,4096]{1,0:T(8,128)(2,1)}), bf16[512,4096]{1,0:T(8,128)(2,1)}) %all-gather.9.cloned.1.call-update) | async-done | bytes 4194320 | tf_op jit(solution)/shard_map/all_gather | solution.py:87
  64.9 3.6 fusion.64
  68.4 1.5 collective-permute-start
  70.0 2.8 collective-permute-done
  74.8 14.3 %all_gather.34 = bf16[4096,64]{0,1:T(8,128)(2,1)S(1)} all-gather(bf16[512,64]{0,1:T(8,128)(2,1)S(1)} %copy-done.15), channel_id=1, replica_groups=mesh['gx'=8,'gy'=16] {'gx'}, dimensions={0}, use_global_device_ids=true | all-gather | bytes 589824 | tf_op jit(solution)/shard_map/all_gather | solution.py:96
  89.1 3.6 fusion.66
  92.7 1.5 collective-permute-start.1
  94.2 2.9 collective-permute-done.1
  97.3 5.4 collective-permute-done.2
  102.8 6.6 %collective-permute-done.3 = bf16[512,128]{0,1:T(8,128)(2,1)S(1)} collective-permute-done((bf16[512,128]{0,1:T(8,128)(2,1)S(1)}, bf16[512,128]{0,1:T(8,128)(2,1)S(1)}, u32[]{:S(2)}, u32[]{:S(2)}) %collective-permute-start.3) | collective-permute-done | bytes 131104 | tf_op jit(solution)/shard_map/ppermute | solution.py:127
  109.4 3.6 fusion.22
  113.6 1.9 collective-permute-done.4
  115.5 1.8 multiply_cosine_fusion
  117.4 3.8 collective-permute-done.5
  121.2 4.2 fusion.65
  125.4 1.5 collective-permute-done.6
  127.3 5.4 collective-permute-done.7
  132.8 1.2 fusion.31
  134.2 7.1 %collective-permute-done.8 = bf16[512,128]{0,1:T(8,128)(2,1)S(1)} collective-permute-done((bf16[512,128]{0,1:T(8,128)(2,1)}, bf16[512,128]{0,1:T(8,128)(2,1)S(1)}, u32[]{:S(2)}, u32[]{:S(2)}) %collective-permute-start.8) | collective-permute-done | bytes 131104 | tf_op jit(solution)/shard_map/ppermute | solution.py:127
  142.0 1.6 constant_dynamic-update-slice_fusion.14
  143.5 1.6 constant_dynamic-update-slice_fusion.13
  149.2 1.6 constant_dynamic-update-slice_fusion.6
  150.8 1.6 constant_dynamic-update-slice_fusion.5
  155.7 27.9 %conditional.1 = (f32[1,2,512]{2,1,0:T(2,128)S(1)}, f32[1,2,512,128]{2,3,1,0:T(8,128)S(1)}) conditional(s32[]{:T(128)} %convert_element_type.117, () %tuple.24, (pred[512,4096]{0,1:T(8,128)(4,1)S(1)}, bf16[512,1,2,128]{3,0,2,1:T(8,128)(2,1)S(1)}, bf16[4096,128]{0,1:T(8,128)(2,1)}, s32[]{:T(128)}, s32[]{:T(128)}, ...), branch_computations={%region_6.7_spmd, %region_7.10_spmd.clone} | conditional | flops 2202008576 | bytes 130834624 | solution.py:159
  155.7 8.6 %fusion = (f32[2,512]{1,0:T(2,128)S(1)}, f32[4096,512,2]{1,0,2:T(8,128)}) fusion(pred[512,4096]{0,1:T(8,128)(4,1)S(1)} %get-tuple-element.113, bf16[512,1,2,128]{3,0,2,1:T(8,128)(2,1)S(1)} %get-tuple-element.115, bf16[4096,128]{0,1:T(8,128)(2,1)} %get-tuple-element.147), kind=kOutput, calls=%fused_computation.2 | convolution fusion | flops 1086323712 | bytes 20189184 | tf_op jit(solution)/shard_map/cond/branch_1_fun/qhgd,khd->hgqk/dot_general | solution.py:140
  164.3 4.1 copy.32
  168.4 8.5 %fusion.7 = f32[1,2,512,128]{2,3,1,0:T(8,128)S(1)} fusion(f32[4096,512,2]{1,0,2:T(8,128)} %get-tuple-element.157, f32[2,512]{1,0:T(2,128)S(1)} %broadcast_maximum_fusion, pred[512,4096]{0,1:T(8,128)(4,1)S(1)} %get-tuple-element.113, bf16[8192,128]{1,0:T(8,128)(2,1)} %copy.32, s32[]{:T(128)S(6)} %select_n.122), kind=kOutput, calls=%fused_computation.8 | convolution fusion | flops 1094713344 | bytes 20451332 | tf_op jit(solution)/shard_map/cond/branch_1_fun/hgqk,khd->hgqd/dot_general | solution.py:151
  176.8 2.4 copy-done
  179.2 4.4 fusion.2
  183.7 4.9 convolution_convert_fusion.1
  189.3 73.6 %reduce-scatter.3.cloned.1.call-done = bf16[32,4096]{1,0:T(8,128)(2,1)} async-done(((bf16[512,4096]{1,0:T(8,128)(2,1)}), bf16[32,4096]{1,0:T(8,128)(2,1)}) %reduce-scatter.3.cloned.1.call-update) | async-done | bytes 262160 | tf_op jit(solution)/shard_map/reduce_scatter | solution.py:167
  262.9 1.1 fusion.27
  264.0 1.8 fusion.29
  267.6 41.9 %all-gather.19.cloned.1.call-done = bf16[4096,896]{1,0:T(8,128)(2,1)} async-done(((bf16[512,896]{1,0:T(8,128)(2,1)}), bf16[4096,896]{1,0:T(8,128)(2,1)}) %all-gather.19.cloned.1.call-update) | async-done | bytes 7340048 | tf_op jit(solution)/shard_map/all_gather | solution.py:177
  309.5 54.3 %all-gather.17.cloned.1.call-done = bf16[512,4096]{1,0:T(8,128)(2,1)} async-done(((bf16[32,4096]{1,0:T(8,128)(2,1)}), bf16[512,4096]{1,0:T(8,128)(2,1)}) %all-gather.17.cloned.1.call-update) | async-done | bytes 4194320 | tf_op jit(solution)/shard_map/all_gather | solution.py:171
  363.9 9.8 %fusion.67 = f32[512,896]{1,0:T(8,128)S(1)} fusion(bf16[512,4096]{1,0:T(8,128)(2,1)} %all-gather.17.cloned.1.call-done, bf16[4096,896]{1,0:T(8,128)(2,1)} %all-gather.19.cloned.1.call-done), kind=kOutput, calls=%fused_computation.138 | convolution fusion | flops 3758096384 | bytes 13369344 | tf_op jit(solution)/shard_map/dot_general | solution.py:58
  373.7 37.3 %all-gather.21.cloned.1.call-done = bf16[4096,896]{1,0:T(8,128)(2,1)} async-done(((bf16[512,896]{1,0:T(8,128)(2,1)}), bf16[4096,896]{1,0:T(8,128)(2,1)}) %all-gather.21.cloned.1.call-update) | async-done | bytes 7340048 | tf_op jit(solution)/shard_map/all_gather | solution.py:178
  410.9 47.3 %all-gather.23.cloned.1.call-done = bf16[896,4096]{1,0:T(8,128)(2,1)} async-done(((bf16[896,512]{1,0:T(8,128)(2,1)}), bf16[896,4096]{1,0:T(8,128)(2,1)}) %all-gather.23.cloned.1.call-update) | async-done | bytes 7340048 | tf_op jit(solution)/shard_map/all_gather | solution.py:182
  458.3 16.3 %convolution_convert_fusion = bf16[512,4096]{1,0:T(8,128)(2,1)} fusion(bf16[896,4096]{1,0:T(8,128)(2,1)} %all-gather.23.cloned.1.call-done, f32[512,896]{1,0:T(8,128)S(1)} %fusion.67, bf16[512,4096]{1,0:T(8,128)(2,1)} %all-gather.17.cloned.1.call-done, bf16[4096,896]{1,0:T(8,128)(2,1)} %all-gather.21.cloned.1.call-done), kind=kOutput, calls=%fused_computation.24 | convolution fusion | flops 7521042432 | bytes 24903680 | tf_op jit(solution)/shard_map/dot_general | solution.py:184
  476.8 0.9 reshape.472
  477.7 3.4 all-to-all-start
  481.1 6.0 %all-to-all-done = bf16[8,2,4096]{2,1,0:T(2,128)(2,1)S(1)} async-done(((bf16[8,2,4096]{2,1,0:T(2,128)(2,1)}), bf16[8,2,4096]{2,1,0:T(2,128)(2,1)S(1)}, u32[]{:S(2)}, u32[]{:S(2)}) %all-to-all-start) | async-done | bytes 131104 | tf_op jit(solution)/shard_map/all_to_all | solution.py:223
  488.0 1.0 reshape.466
  489.0 63.3 %reduce-scatter.5.cloned.1.call-done = bf16[32,4096]{1,0:T(8,128)(2,1)} async-done(((bf16[512,4096]{1,0:T(8,128)(2,1)}), bf16[32,4096]{1,0:T(8,128)(2,1)}) %reduce-scatter.5.cloned.1.call-update) | async-done | bytes 262160 | tf_op jit(solution)/shard_map/reduce_scatter | solution.py:183
  552.3 1.7 fusion.30
  (122 shorter events, 19.6 us)
Async XLA Ops:
  7.2 57.7 %all-gather.9.cloned.1.call-start = ((), (), s32[]{:S(2)}) async-start(), calls=%async_computation.3 | async-start | bytes 4456448 | tf_op jit(solution)/shard_map/all_gather | solution.py:87
  10.8 110.3 %all-gather.11.cloned.1.call-start = ((), (), s32[]{:S(2)}) async-start(), calls=%async_computation.4 | async-start | bytes 2359296 | tf_op jit(solution)/shard_map/all_gather | solution.py:90
  11.6 144.1 %all-gather.13.cloned.1.call-start = ((), (), s32[]{:S(2)}) async-start(), calls=%async_computation.5 | async-start | bytes 1179648 | tf_op jit(solution)/shard_map/all_gather | solution.py:124
  27.9 46.9 %copy-start.15 = (bf16[512,64]{0,1:T(8,128)(2,1)S(1)}, bf16[512,64]{0,1:T(8,128)(2,1)}, u32[]{:S(2)}) copy-start(bf16[512,64]{0,1:T(8,128)(2,1)} %param.19) | copy-start | bytes 196612
  68.4 4.3 collective-permute-start
  73.4 0.6 copy-start.3
  73.4 0.7 copy-start.5
  74.7 109.0 %all-gather.15.cloned.1.call-start = ((), (), s32[]{:S(2)}) async-start(), calls=%async_computation.6 | async-start | bytes 2359296 | tf_op jit(solution)/shard_map/all_gather | solution.py:164
  92.7 4.4 collective-permute-start.1
  97.1 5.6 %collective-permute-start.2 = (bf16[512,128]{0,1:T(8,128)(2,1)S(1)}, bf16[512,128]{0,1:T(8,128)(2,1)S(1)}, u32[]{:S(2)}, u32[]{:S(2)}) collective-permute-start(bf16[512,128]{0,1:T(8,128)(2,1)S(1)} %fusion.33), channel_id=1, source_target_pairs={{0,16},{16,32},{32,48},{48,64},{64,80},{80,96},{96,112},{112,0},{1... | collective-permute-start | bytes 393224 | tf_op jit(solution)/shard_map/ppermute | solution.py:127
  97.2 165.7 %reduce-scatter.3.cloned.1.call-start = ((), (), s32[]{:S(2)}) async-start(), calls=%async_computation.7 | async-start | bytes 4456448 | tf_op jit(solution)/shard_map/reduce_scatter | solution.py:167
  102.7 6.7 %copy-start.7 = (bf16[512,128]{0,1:T(8,128)(2,1)}, bf16[512,128]{0,1:T(8,128)(2,1)S(1)}, u32[]{:S(2)}) copy-start(bf16[512,128]{0,1:T(8,128)(2,1)S(1)} %collective-permute-done.2) | copy-start | bytes 393220
  102.7 6.7 %collective-permute-start.3 = (bf16[512,128]{0,1:T(8,128)(2,1)S(1)}, bf16[512,128]{0,1:T(8,128)(2,1)S(1)}, u32[]{:S(2)}, u32[]{:S(2)}) collective-permute-start(bf16[512,128]{0,1:T(8,128)(2,1)S(1)} %collective-permute-done.2), channel_id=1, source_target_pairs={{0,16},{16,32},{32,48},{48,64},{64,80},{80,96},{96,112},{112,0},{1... | collective-permute-start | bytes 393224 | tf_op jit(solution)/shard_map/ppermute | solution.py:127
  109.4 11.7 %copy-start.9 = (bf16[512,128]{0,1:T(8,128)(2,1)}, bf16[512,128]{0,1:T(8,128)(2,1)S(1)}, u32[]{:S(2)}) copy-start(bf16[512,128]{0,1:T(8,128)(2,1)S(1)} %collective-permute-done.3) | copy-start | bytes 393220
  109.4 6.1 %collective-permute-start.4 = (bf16[512,128]{0,1:T(8,128)(2,1)S(1)}, bf16[512,128]{0,1:T(8,128)(2,1)S(1)}, u32[]{:S(2)}, u32[]{:S(2)}) collective-permute-start(bf16[512,128]{0,1:T(8,128)(2,1)S(1)} %collective-permute-done.3), channel_id=1, source_target_pairs={{0,16},{16,32},{32,48},{48,64},{64,80},{80,96},{96,112},{112,0},{1... | collective-permute-start | bytes 393224 | tf_op jit(solution)/shard_map/ppermute | solution.py:127
  115.5 5.6 %copy-start.11 = (bf16[512,128]{0,1:T(8,128)(2,1)}, bf16[512,128]{0,1:T(8,128)(2,1)S(1)}, u32[]{:S(2)}) copy-start(bf16[512,128]{0,1:T(8,128)(2,1)S(1)} %collective-permute-done.4) | copy-start | bytes 393220
  115.5 5.6 collective-permute-start.5
  121.1 4.2 copy-start.13
  121.1 5.7 %collective-permute-start.6 = (bf16[512,128]{0,1:T(8,128)(2,1)S(1)}, bf16[512,128]{0,1:T(8,128)(2,1)}, u32[]{:S(2)}, u32[]{:S(2)}) collective-permute-start(bf16[512,128]{0,1:T(8,128)(2,1)S(1)} %collective-permute-done.5), channel_id=1, source_target_pairs={{0,16},{16,32},{32,48},{48,64},{64,80},{80,96},{96,112},{112,0},{1... | collective-permute-start | bytes 393224 | tf_op jit(solution)/shard_map/ppermute | solution.py:127
  126.9 5.9 %collective-permute-start.7 = (bf16[512,128]{0,1:T(8,128)(2,1)}, bf16[512,128]{0,1:T(8,128)(2,1)}, u32[]{:S(2)}, u32[]{:S(2)}) collective-permute-start(bf16[512,128]{0,1:T(8,128)(2,1)} %collective-permute-done.6), channel_id=1, source_target_pairs={{0,16},{16,32},{32,48},{48,64},{64,80},{80,96},{96,112},{112,0},{1... | collective-permute-start | bytes 393224 | tf_op jit(solution)/shard_map/ppermute | solution.py:127
  127.3 17.8 %copy-start.14 = (bf16[512,128]{0,1:T(8,128)(2,1)S(1)}, bf16[512,128]{0,1:T(8,128)(2,1)}, u32[]{:S(2)}) copy-start(bf16[512,128]{0,1:T(8,128)(2,1)} %copy-done.13) | copy-start | bytes 393220
  127.3 18.5 %copy-start.12 = (bf16[512,128]{0,1:T(8,128)(2,1)S(1)}, bf16[512,128]{0,1:T(8,128)(2,1)}, u32[]{:S(2)}) copy-start(bf16[512,128]{0,1:T(8,128)(2,1)} %copy-done.11) | copy-start | bytes 393220
  132.8 8.5 %collective-permute-start.8 = (bf16[512,128]{0,1:T(8,128)(2,1)}, bf16[512,128]{0,1:T(8,128)(2,1)S(1)}, u32[]{:S(2)}, u32[]{:S(2)}) collective-permute-start(bf16[512,128]{0,1:T(8,128)(2,1)} %collective-permute-done.7), channel_id=1, source_target_pairs={{0,16},{16,32},{32,48},{48,64},{64,80},{80,96},{96,112},{112,0},{1... | collective-permute-start | bytes 393224 | tf_op jit(solution)/shard_map/ppermute | solution.py:127
  132.8 13.7 %copy-start.10 = (bf16[512,128]{0,1:T(8,128)(2,1)S(1)}, bf16[512,128]{0,1:T(8,128)(2,1)}, u32[]{:S(2)}) copy-start(bf16[512,128]{0,1:T(8,128)(2,1)} %copy-done.9) | copy-start | bytes 393220
  132.8 14.4 %copy-start.8 = (bf16[512,128]{0,1:T(8,128)(2,1)S(1)}, bf16[512,128]{0,1:T(8,128)(2,1)}, u32[]{:S(2)}) copy-start(bf16[512,128]{0,1:T(8,128)(2,1)} %copy-done.7) | copy-start | bytes 393220
  168.4 10.8 %copy-start = (f32[4096,512,2]{1,0,2:T(8,128)S(1)}, f32[4096,512,2]{1,0,2:T(8,128)}, u32[]{:S(2)}) copy-start(f32[4096,512,2]{1,0,2:T(8,128)} %get-tuple-element.157) | copy-start | bytes 50331652 | tf_op jit(solution)/shard_map/cond
  188.6 0.7 copy-start.16
  188.6 74.3 %copy-start.1 = (bf16[32,4096]{1,0:T(8,128)(2,1)S(1)}, bf16[32,4096]{1,0:T(8,128)(2,1)}, u32[]{:S(2)}) copy-start(bf16[32,4096]{1,0:T(8,128)(2,1)} %param.14) | copy-start | bytes 786436
  188.7 120.9 %all-gather.19.cloned.1.call-start = ((), (), s32[]{:S(2)}) async-start(), calls=%async_computation.9 | async-start | bytes 8257536 | tf_op jit(solution)/shard_map/all_gather | solution.py:177
  189.2 174.6 %all-gather.17.cloned.1.call-start = ((), (), s32[]{:S(2)}) async-start(), calls=%async_computation.8 | async-start | bytes 4456448 | tf_op jit(solution)/shard_map/all_gather | solution.py:171
  265.8 145.1 %all-gather.21.cloned.1.call-start = ((), (), s32[]{:S(2)}) async-start(), calls=%async_computation.10 | async-start | bytes 8257536 | tf_op jit(solution)/shard_map/all_gather | solution.py:178
  266.6 191.7 %all-gather.23.cloned.1.call-start = ((), (), s32[]{:S(2)}) async-start(), calls=%async_computation.11 | async-start | bytes 8257536 | tf_op jit(solution)/shard_map/all_gather | solution.py:182
  267.3 284.9 %reduce-scatter.5.cloned.1.call-start = ((), (), s32[]{:S(2)}) async-start(), calls=%async_computation.12 | async-start | bytes 4456448 | tf_op jit(solution)/shard_map/reduce_scatter | solution.py:183
  474.6 0.7 copy-start.17
  474.6 1.0 copy-start.4
  474.6 1.0 copy-start.6
  476.0 76.3 %copy-start.2 = (bf16[32,4096]{1,0:T(8,128)(2,1)S(1)}, bf16[32,4096]{1,0:T(8,128)(2,1)}, u32[]{:S(2)}) copy-start(bf16[32,4096]{1,0:T(8,128)(2,1)} %reduce-scatter.3.cloned.1.call-done) | copy-start | bytes 786436
  477.7 9.4 %all-to-all-start = ((bf16[8,2,4096]{2,1,0:T(2,128)(2,1)}), bf16[8,2,4096]{2,1,0:T(2,128)(2,1)S(1)}, u32[]{:S(2)}, u32[]{:S(2)}) async-start(bf16[8,2,4096]{2,1,0:T(2,128)(2,1)} %reshape.472), calls=%async_computation.2 | async-start | bytes 262144 | tf_op jit(solution)/shard_map/all_to_all | solution.py:223
Sparse Core Ops, SparseCore 0:
  11.0 53.8 all-gather.8
  66.6 25.9 all-gather.10
  94.2 24.0 all-gather.12
  119.9 25.1 all-gather.14
  188.8 74.0 reduce-scatter.2
  264.5 44.9 all-gather.18
  312.5 51.3 all-gather.16
  365.7 45.2 all-gather.20
  412.8 45.4 all-gather.22
  474.7 77.5 reduce-scatter.4
